TPU v7x, 256 devices: a whole 4x4x8 slice. The times are simulated.
256 devices in a mesh: blk: 64 (over x, z, core), tm: 4 (over y).
Axes of the slice: x: 4, y: 4, z: 8, core: 2. Of those that a mesh axis runs over, the one named last changes fastest.
Arguments:
- density: bfloat16 [6144, 256, 128], P('blk', 'tm'), may hold values from 0.5 to 2
- flow_rest: bfloat16 [6144, 4, 256, 128], P('blk', None, 'tm'), may hold values from -6 to 6
- dest: int32 [6144, 1], P('blk'), may hold values from 0 to 63; in each aligned block of 96 rows (0 to 95, 96 to 191, ...) at most 4 rows name the same one
- weights: bfloat16 [64, 64, 256, 128], P('blk', None, 'tm'), may hold values from -0.001953125 to 0.001953125
- directions: float32 [64, 3], replicated, may hold values from -4 to 4
- bins: int32 [64, 64], P(None, 'blk'), may hold values from 0 to 255
Outputs:
- record: float32 [64, 256], P('blk', 'tm')
Inputs may be any that keep to these rules, and one draw needn't show every extreme that they name: `dest`: each row names one source block; the rows of one partition name any block at most 4 times, and some partition names some block exactly 4 times.
All inputs are finite; a program needn't handle non-finite values.
Results may differ from a plain program's by a relative error of at most 0.0003.
Values may be sent and summed in bfloat16 or wider, within the bound.
A program may use at most 128 MiB of HBM per device.

v0:
```python
import jax
import jax.numpy as jnp
from jax import lax
from jax.sharding import PartitionSpec as P


def stress_terms(density, flow_rest):
    rho = density.astype(jnp.float32)
    speed_x = flow_rest[..., 0, :, :].astype(jnp.float32)
    speed_y = flow_rest[..., 1, :, :].astype(jnp.float32)
    speed_z = flow_rest[..., 2, :, :].astype(jnp.float32)
    excess = flow_rest[..., 3, :, :].astype(jnp.float32)
    pieces = [
        rho * speed_x * speed_x + excess,
        rho * speed_y * speed_y + excess,
        rho * speed_z * speed_z + excess,
        rho * speed_x * speed_y,
        rho * speed_x * speed_z,
        rho * speed_y * speed_z,
    ]
    pieces = [jnp.sum(term, axis=0) for term in pieces]
    return jnp.stack(pieces, axis=-3)


def slot_sums(pieces):
    return stress_terms(pieces[0], pieces[1])


def body(density, flow_rest, dest, weights, directions, bins):
    row_count = density.shape[0]
    slab_len = density.shape[1]
    cells = density.shape[2]
    blocks = lax.axis_size("blk")
    capacity = max(4, 2 * row_count // blocks)
    targets = dest[:, 0]
    onehot = (targets[:, None] == jnp.arange(blocks, dtype=jnp.int32)[None, :]).astype(jnp.int32)
    before = jnp.cumsum(onehot, axis=0) - onehot
    order_in = jnp.sum(before * onehot, axis=1)
    position = targets * capacity + order_in
    send_dens = (
        jnp.zeros((blocks * capacity, slab_len, cells), jnp.bfloat16).at[position].set(density)
    )
    send_dens = send_dens.reshape(blocks, capacity, slab_len, cells)
    send_flow = (
        jnp.zeros((blocks * capacity, 4, slab_len, cells), jnp.bfloat16).at[position].set(flow_rest)
    )
    send_flow = send_flow.reshape(blocks, capacity, 4, slab_len, cells)
    partials = slot_sums(
        (
            lax.all_to_all(send_dens, "blk", split_axis=0, concat_axis=0, tiled=True),
            lax.all_to_all(send_flow, "blk", split_axis=0, concat_axis=0, tiled=True),
        )
    )
    totals = jnp.sum(partials, axis=0)
    projector = jnp.stack(
        [
            directions[:, 0] * directions[:, 0],
            directions[:, 1] * directions[:, 1],
            directions[:, 2] * directions[:, 2],
            2.0 * directions[:, 0] * directions[:, 1],
            2.0 * directions[:, 0] * directions[:, 2],
            2.0 * directions[:, 1] * directions[:, 2],
        ],
        axis=1,
    )
    moment = jnp.einsum("oi,itc->otc", projector, totals, precision=lax.Precision.HIGHEST)
    source = jnp.sum(weights[0].astype(jnp.float32) * moment, axis=2)
    period = lax.all_gather(source, "tm", axis=1, tiled=True)
    steps_total = period.shape[1]
    curved = jnp.roll(period, -1, axis=1) - 2.0 * period + jnp.roll(period, 1, axis=1)
    out_times = lax.axis_index("tm") * slab_len + jnp.arange(slab_len, dtype=jnp.int32)
    lagged = jnp.mod(out_times[None, :] - bins, steps_total)
    shifted = jnp.take_along_axis(curved, lagged, axis=1)
    return lax.psum_scatter(shifted, "blk", scatter_dimension=0, tiled=True)


def solution(mesh):
    placed = (
        P("blk", "tm", None),
        P("blk", None, "tm", None),
        P("blk", None),
        P("blk", None, "tm", None),
        P(),
        P(None, "blk"),
    )
    return jax.shard_map(
        body, mesh=mesh, in_specs=placed, out_specs=P("blk", "tm"), check_vma=False
    )
```

profile of v0, /device:TPU:1, one launch (start us, length us, event | category | flops | bytes accessed | tf_op | source)
XLA Modules:
  0.0 798.7 jit_solution(2754499571994074604)
XLA Ops:
  0.0 0.8 fusion.9
  0.9 0.1 reduce_window_sum.11
  1.0 0.8 select_reduce_fusion
  1.8 0.7 fusion.16
  2.5 3.0 broadcast_in_dim.14
  5.5 0.0 copy-done
  5.5 11.9 %scatter_fusion = bf16[256,64,128]{2,1,0:T(8,128)(2,1)} fusion(bf16[256,64,128]{2,1,0:T(8,128)(2,1)} %broadcast_in_dim.14, s32[96]{0:T(128)S(1)} %fusion.16, bf16[96,64,128]{2,1,0:T(8,128)(2,1)S(1)} %copy-done), kind=kCustom, calls=%fused_computation.1 | custom fusion | bytes 4718976 | tf_op jit(solution)/shard_map/scatter | solution.py:41
  17.4 13.1 %all-to-all-start = ((bf16[64,4,64,128]{3,2,1,0:T(8,128)(2,1)}), bf16[64,4,64,128]{3,2,1,0:T(8,128)(2,1)}, u32[]{:S(2)}, u32[]{:S(2)}) async-start(bf16[64,4,64,128]{3,2,1,0:T(8,128)(2,1)} %bitcast.74), calls=%async_computation | async-start | bytes 8388608 | tf_op jit(solution)/shard_map/all_to_all | solution.py:50
  30.6 6.4 broadcast_in_dim.15
  37.0 17.7 %scatter_fusion.1 = bf16[256,4,64,128]{3,2,1,0:T(8,128)(2,1)} fusion(bf16[256,4,64,128]{3,2,1,0:T(8,128)(2,1)} %broadcast_in_dim.15, s32[96]{0:T(128)S(1)} %fusion.16, bf16[96,4,64,128]{3,2,1,0:T(8,128)(2,1)} %param.7), kind=kCustom, calls=%fused_computation.2 | custom fusion | bytes 18874752 | tf_op jit(solution)/shard_map/scatter | solution.py:45
  54.6 14.1 %copy.21 = bf16[64,4,4,64,128]{4,3,1,2,0:T(8,128)(2,1)} copy(bf16[64,4,4,64,128]{4,3,2,1,0:T(8,128)(2,1)} %bitcast.73) | data formatting | bytes 33554432 | tf_op jit(solution)/shard_map/reshape | solution.py:47
  68.7 57.7 %all-to-all-done = bf16[64,4,64,128]{3,2,1,0:T(8,128)(2,1)} async-done(((bf16[64,4,64,128]{3,2,1,0:T(8,128)(2,1)}), bf16[64,4,64,128]{3,2,1,0:T(8,128)(2,1)}, u32[]{:S(2)}, u32[]{:S(2)}) %all-to-all-start) | async-done | bytes 4194336 | tf_op jit(solution)/shard_map/all_to_all | solution.py:50
  126.4 5.9 all-to-all-start.1
  132.4 0.1 fusion.14
  132.5 0.1 reshape.138
  132.6 0.6 dynamic-slice
  133.2 0.0 copy-start.3
  133.2 364.7 %all-to-all-done.1 = bf16[64,4,4,64,128]{4,3,1,2,0:T(8,128)(2,1)} async-done(((bf16[64,4,4,64,128]{4,3,1,2,0:T(8,128)(2,1)}), bf16[64,4,4,64,128]{4,3,1,2,0:T(8,128)(2,1)}, u32[]{:S(2)}, u32[]{:S(2)}) %all-to-all-start.1) | async-done | bytes 16777248 | tf_op jit(solution)/shard_map/all_to_all | solution.py:51
  497.9 10.5 %fusion.5 = (f32[4,64,128]{2,1,0:T(8,128)S(1)}, f32[4,64,128]{2,1,0:T(8,128)S(1)}, f32[4,64,128]{2,1,0:T(8,128)S(1)}, f32[4,64,128]{2,1,0:T(8,128)S(1)}, f32[4,6...) fusion(bf16[64,4,64,128]{3,2,1,0:T(8,128)(2,1)} %all-to-all-done, bf16[64,4,4,64,128]{4,3,1,2,0:T(8,128)(2,1)} %all-to-all-done.1), kind=kLoop, calls=%fused_computation.20 | loop fusion | flops 48037888 | bytes 21757952 | tf_op jit(solution)/shard_map/reduce_sum | solution.py:21
  508.6 0.0 copy-done.3
  508.6 2.8 fusion.6
  511.4 9.9 %all_gather.3 = f32[64,256]{0,1:T(8,128)S(1)} all-gather(f32[64,64]{0,1:T(8,128)S(1)} %fusion.6), channel_id=1, replica_groups=mesh['blk'=64,'tm'=4] {'tm'}, dimensions={1}, use_global_device_ids=true | all-gather | bytes 81920 | tf_op jit(solution)/shard_map/all_gather | solution.py:68
  521.3 0.1 copy.26
  521.4 0.1 fusion.18
  521.5 0.1 copy.27
  521.6 0.1 copy.30
  521.7 0.1 fusion.8
  521.8 32.8 %gather_fusion = f32[4096]{0:T(1024)S(1)} fusion(f32[64,256]{1,0:T(8,128)S(1)} %fusion.8, s32[4096]{0:T(1024)S(1)} %reshape.138), kind=kCustom, calls=%fused_computation | custom fusion | bytes 65536 | tf_op jit(solution)/shard_map/jit(take_along_axis)/gather | solution.py:73
  554.6 0.1 reshape.141
  554.7 0.1 and_select_fusion
  554.8 242.8 %all-reduce = f32[64,64]{1,0:T(8,128)S(1)} all-reduce(f32[64,64]{1,0:T(8,128)S(1)} %and_select_fusion), channel_id=2, replica_groups=mesh['blk'=64,'tm'=4] {'blk'}, use_global_device_ids=true, to_apply=%region_12.13.clone | all-reduce | flops 4096 | bytes 32768
  797.5 1.1 constant_dynamic-slice_fusion
  (18 shorter events, 0.2 us)
Async XLA Ops:
  0.0 5.5 copy-start
  17.4 109.0 %all-to-all-start = ((bf16[64,4,64,128]{3,2,1,0:T(8,128)(2,1)}), bf16[64,4,64,128]{3,2,1,0:T(8,128)(2,1)}, u32[]{:S(2)}, u32[]{:S(2)}) async-start(bf16[64,4,64,128]{3,2,1,0:T(8,128)(2,1)} %bitcast.74), calls=%async_computation | async-start | bytes 8388608 | tf_op jit(solution)/shard_map/all_to_all | solution.py:50
  68.7 63.7 %copy-start.1 = (s32[64,1]{0,1:T(1,128)S(1)}, s32[64,1]{0,1:T(1,128)}, u32[]{:S(2)}) copy-start(s32[64,1]{0,1:T(1,128)} %param.11) | copy-start | bytes 772
  68.7 63.9 %copy-start.4 = (u32[256]{0:T(256)S(1)}, u32[256]{0:T(256)}, u32[]{:S(2)}) copy-start(u32[256]{0:T(256)} %constant.73) | copy-start | bytes 3076
  68.7 64.5 %copy-start.2 = (f32[64,3]{0,1:T(4,128)S(1)}, f32[64,3]{0,1:T(4,128)}, u32[]{:S(2)}) copy-start(f32[64,3]{0,1:T(4,128)} %param.10) | copy-start | bytes 2308
  126.4 371.4 %all-to-all-start.1 = ((bf16[64,4,4,64,128]{4,3,1,2,0:T(8,128)(2,1)}), bf16[64,4,4,64,128]{4,3,1,2,0:T(8,128)(2,1)}, u32[]{:S(2)}, u32[]{:S(2)}) async-start(bf16[64,4,4,64,128]{4,3,1,2,0:T(8,128)(2,1)} %copy.21), calls=%async_computation.1 | async-start | bytes 33554432 | tf_op jit(solution)/shard_map/all_to_all | solution.py:51
  133.2 375.4 %copy-start.3 = (bf16[1,64,64,128]{3,2,1,0:T(8,128)(2,1)S(1)}, bf16[1,64,64,128]{3,2,1,0:T(8,128)(2,1)}, u32[]{:S(2)}) copy-start(bf16[1,64,64,128]{3,2,1,0:T(8,128)(2,1)} %param.9) | copy-start | bytes 3145732
where the time goes:
time: 804 us; the launch traced here: 799 us
  waiting for transfers between devices  422 us (52%)
  blocking collectives  253 us (31%)
  local copies, waits for them, and re-layouts  88.2 us (11%)
  starting transfers between devices  19.1 us (2%)
  other arithmetic  13.4 us (2%)
    all_to_all x1, waiting for transfers between devices, body(): lax.all_to_all(send_flow, 'blk', split_axis=0, concat_axis=0, tiled=True)  365 us
    unnamed x1, blocking collectives  243 us
    all_to_all x1, waiting for transfers between devices, body(): lax.all_to_all(send_dens, 'blk', split_axis=0, concat_axis=0, tiled=True)  57.7 us
    gather x3, local copies, waits for them, and re-layouts, body(): shifted = jnp.take_along_axis(curved, lagged, axis=1)  32.9 us
    scatter x1, local copies, waits for them, and re-layouts, body(): jnp.zeros((blocks * capacity, 4, slab_len, cells), jnp.bfloat16)  17.7 us
  transfers between devices with their start and end apart: 2, of which 2 were waited for; matrix products, arithmetic and copies ran while one was open for 5% of the time, Pallas kernels for 0%

commit v1 on v0

v1 whole, which is shorter than its diff:
```python
import functools

import jax
import jax.numpy as jnp
from jax import lax
from jax.experimental import pallas as pl
from jax.experimental.pallas import tpu as pltpu
from jax.sharding import PartitionSpec as P

NX, NZ, NY = 4, 8, 4
ROWS_DEV = 96
SLOTS = 4
NA = 7
NB = 12 - NA
TILES = [(0, i) for i in range(6)] + [(1, i) for i in (5, 4, 3, 2, 1, 0)]
A0, A1, A2 = 0, NA, 2 * NA
B0, B1, B2 = 2 * NA, 2 * NA + NB, 2 * NA + 2 * NB
MESH = pl.DeviceIdType.MESH


def place(j, tile):
    if tile < NA:
        return j * NA + tile
    return 2 * NA + j * NB + tile - NA


def far_first(i, n):
    step = (i + 1) // 2
    return (n // 2 + step * (1 - 2 * (i % 2))) % n


def prep_kernel(dest_ref, bins_ref, list_ref, lag_ref):
    dest = jnp.broadcast_to(dest_ref[...], (ROWS_DEV, 128))
    lane = lax.broadcasted_iota(jnp.int32, (ROWS_DEV, 128), 1)
    row = lax.broadcasted_iota(jnp.int32, (ROWS_DEV, 128), 0)
    hit = dest == lane
    earlier = (
        lax.broadcasted_iota(jnp.int32, (ROWS_DEV, ROWS_DEV), 0)
        > lax.broadcasted_iota(jnp.int32, (ROWS_DEV, ROWS_DEV), 1)
    ).astype(jnp.bfloat16)
    before = jnp.dot(
        earlier, hit.astype(jnp.bfloat16), preferred_element_type=jnp.float32
    ).astype(jnp.int32)
    for s in range(8):
        chosen = jnp.where(hit & (before == s), row, ROWS_DEV)
        list_ref[pl.ds(s, 1), :] = jnp.min(chosen, axis=0, keepdims=True)
    bins = jnp.broadcast_to(bins_ref[...], (64, 128))
    lane64 = lax.broadcasted_iota(jnp.int32, (64, 128), 1) % 64
    row64 = lax.broadcasted_iota(jnp.int32, (64, 128), 0)
    lags = jnp.sum(jnp.where(lane64 == row64, bins, 0), axis=0, keepdims=True)
    lag_ref[...] = jnp.broadcast_to(lags, (8, 128))


def main_kernel(
    list_ref, dir_ref, lag_ref, dens_hbm, flow_hbm, wts_hbm, out_ref,
    dens, flow, C, S, R0, RA1, RA2, RA3, RA4, RB1, RB2, RB3, RB4, W, lag2, G, M, HS, HR,
    ld_sem, s0, r0, sa1, ra1, sa2, ra2, sa3, ra3, sa4, ra4,
    sb1, rb1, sb2, rb2, sb3, rb3, sb4, rb4, sw, rw, sl, rl, sg, rg, sh, rh,
):
    blk = lax.axis_index("blk")
    yy = lax.axis_index("tm")
    c = blk % 2
    chip = blk // 2
    z = chip % NZ
    x = chip // NZ

    def dev(dx, dz, core):
        return (((x + dx) % NX) * NZ + (z + dz) % NZ) * 2 + core

    near_x = (dev(1, 0, c), dev(NX - 1, 0, c))
    near_z = (dev(0, 1, c), dev(0, NZ - 1, c))
    mate = dev(0, 0, 1 - c)

    def remote(src, dst, ssem, rsem, to, ty=None):
        return pltpu.make_async_remote_copy(
            src_ref=src, dst_ref=dst, send_sem=ssem, recv_sem=rsem,
            device_id=(to, yy if ty is None else ty), device_id_type=MESH,
        )

    loads = [
        pltpu.make_async_copy(dens_hbm, dens.at[pl.ds(0, ROWS_DEV)], ld_sem.at[0]),
        pltpu.make_async_copy(flow_hbm, flow.at[pl.ds(0, ROWS_DEV)], ld_sem.at[1]),
        pltpu.make_async_copy(
            wts_hbm.at[0, :, pl.ds(pl.multiple_of(c * 32, 32), 32), :], W.at[c], ld_sem.at[2]
        ),
    ]
    for copy in loads:
        copy.start()

    barrier = pltpu.get_barrier_semaphore()
    for to in near_x + near_z + (mate,):
        pl.semaphore_signal(barrier, inc=1, device_id=(to, yy), device_id_type=MESH)
    for dy in range(1, NY):
        for core in range(2):
            pl.semaphore_signal(
                barrier, inc=1, device_id=(chip * 2 + core, (yy + dy) % NY), device_id_type=MESH
            )
    pl.semaphore_wait(barrier, 5 + 2 * (NY - 1))

    wts_copy = remote(
        wts_hbm.at[0, :, pl.ds(pl.multiple_of((1 - c) * 32, 32), 32), :], W.at[c], sw, rw, mate
    )
    lag_copy = remote(lag_ref, lag2, sl, rl, mate)

    dens[ROWS_DEV] = jnp.zeros((64, 128), jnp.bfloat16)
    flow[ROWS_DEV] = jnp.zeros((4, 64, 128), jnp.bfloat16)
    loads[0].wait()
    loads[1].wait()

    def core_copy(dx, dz):
        return remote(S.at[dx, dz], R0.at[dx, dz], s0.at[dx, dz], r0.at[dx, dz], mate)

    def unit(dx, dz):
        first = dev(dx, dz, 0)
        for j in range(2):
            rows = [list_ref[s, first + j] for s in range(SLOTS)]
            for part in range(2):
                target = C if part == 0 else S
                for chunk in range(2):
                    off = pl.multiple_of(((c + part) % 2) * 32 + chunk * 16, 16)
                    span = pl.ds(off, 16)
                    acc = None
                    for r in rows:
                        rho = dens[r, span, :].astype(jnp.float32)
                        u = flow[r, 0, span, :].astype(jnp.float32)
                        v = flow[r, 1, span, :].astype(jnp.float32)
                        w = flow[r, 2, span, :].astype(jnp.float32)
                        e = flow[r, 3, span, :].astype(jnp.float32)
                        ru, rv, rw_ = rho * u, rho * v, rho * w
                        terms = [ru * u, rv * v, rw_ * w, ru * v, ru * w, rv * w, e]
                        acc = terms if acc is None else [p + q for p, q in zip(acc, terms)]
                    sums = [acc[0] + acc[6], acc[1] + acc[6], acc[2] + acc[6], acc[3], acc[4], acc[5]]
                    for tile, (ch, comp) in enumerate(TILES):
                        if ch == chunk:
                            target[dx, dz, place(j, tile)] = sums[comp]
        core_copy(dx, dz).start()

    def add(dx, dz, lo, hi, *others):
        span = pl.ds(lo, hi - lo)
        total = C[dx, dz, span]
        for ref in others:
            total = total + ref[...]
        C[dx, dz, span] = total

    half_a = ((A0, A1), (A1, A2))
    half_b = ((B0, B1), (B1, B2))

    def src(dx, dz, lo, hi):
        return C.at[dx, dz, pl.ds(lo, hi - lo)]

    def m_a1(d, dz):
        return remote(src(2, dz, *half_a[d]), RA1.at[d, dz], sa1.at[d, dz], ra1.at[d, dz], near_x[d])

    def m_a2(d, dz):
        return remote(src(1 if d == 0 else 3, dz, A0, A2), RA2.at[d, dz], sa2.at[d, dz], ra2.at[d, dz], near_x[d])

    def m_a3(d):
        return remote(src(0, 4, *half_a[d]), RA3.at[d], sa3.at[d], ra3.at[d], near_z[d])

    def m_a4(d, k):
        dz = 3 - k if d == 0 else 5 + k
        return remote(src(0, dz, A0, A2), RA4.at[d, k], sa4.at[d, k], ra4.at[d, k], near_z[d])

    def m_b1(d, dx):
        return remote(src(dx, 4, *half_b[d]), RB1.at[d, dx], sb1.at[d, dx], rb1.at[d, dx], near_z[d])

    def m_b2(d, k, dx):
        dz = 3 - k if d == 0 else 5 + k
        return remote(src(dx, dz, B0, B2), RB2.at[d, k, dx], sb2.at[d, k, dx], rb2.at[d, k, dx], near_z[d])

    def m_b3(d):
        return remote(src(2, 0, *half_b[d]), RB3.at[d], sb3.at[d], rb3.at[d], near_x[d])

    def m_b4(d):
        return remote(src(1 if d == 0 else 3, 0, B0, B2), RB4.at[d], sb4.at[d], rb4.at[d], near_x[d])

    def finish(gp):
        dz = far_first(gp, NZ)

        def step(k, carry):
            dx = far_first(k, NX)
            core_copy(dx, dz).wait_recv()
            add(dx, dz, 0, 24, R0.at[dx, dz])

            @pl.when(k == 0)
            def _():
                m_a1(0, dz).start()
                m_a1(1, dz).start()

            @pl.when(gp == 0)
            def _():
                m_b1(0, dx).start()
                m_b1(1, dx).start()

            return carry

        lax.fori_loop(0, NX, step, 0)

    def ev_a2(dz):
        for d in range(2):
            m_a1(d, dz).wait_recv()
            add(1 if d == 0 else 3, dz, *half_a[d], RA1.at[d, dz])
            m_a2(d, dz).start()

    def ev_b2(k, dx):
        for d in range(2):
            dz = 3 - k if d == 0 else 5 + k
            if k == 0:
                m_b1(d, dx).wait_recv()
                add(dx, dz, *half_b[d], RB1.at[d, dx])
            else:
                m_b2(d, k - 1, dx).wait_recv()
                add(dx, dz, B0, B2, RB2.at[d, k - 1, dx])
            m_b2(d, k, dx).start()

    def ev_ra2(dz):
        m_a2(0, dz).wait_recv()
        m_a2(1, dz).wait_recv()
        add(0, dz, A0, A2, RA2.at[0, dz], RA2.at[1, dz])
        if dz == 4:
            m_a3(0).start()
            m_a3(1).start()
        elif dz == 0:
            m_a4(0, 2).wait_recv()
            m_a4(1, 2).wait_recv()
            add(0, 0, A0, A2, RA4.at[0, 2], RA4.at[1, 2])
        else:
            d, k = (0, 3 - dz) if dz < 4 else (1, dz - 5)
            if k == 0:
                m_a3(d).wait_recv()
                add(0, dz, *half_a[d], RA3.at[d])
            else:
                m_a4(d, k - 1).wait_recv()
                add(0, dz, A0, A2, RA4.at[d, k - 1])
            m_a4(d, k).start()

    def ev_rb2(dx):
        m_b2(0, 2, dx).wait_recv()
        m_b2(1, 2, dx).wait_recv()
        add(dx, 0, B0, B2, RB2.at[0, 2, dx], RB2.at[1, 2, dx])
        if dx == 2:
            m_b3(0).start()
            m_b3(1).start()
        elif dx == 0:
            m_b4(0).wait_recv()
            m_b4(1).wait_recv()
            add(0, 0, B0, B2, RB4.at[0], RB4.at[1])
        else:
            d = 0 if dx == 1 else 1
            m_b3(d).wait_recv()
            add(dx, 0, *half_b[d], RB3.at[d])
            m_b4(d).start()

    def group(g, carry):
        dz = far_first(g, NZ)

        def step(k, inner):
            unit(far_first(k, NX), dz)
            return inner

        lax.fori_loop(0, NX, step, 0)

        @pl.when(g >= 1)
        def _():
            finish(g - 1)

        @pl.when(g == 3)
        def _():
            def send(k, inner):
                ev_b2(0, far_first(k, NX))
                return inner

            lax.fori_loop(0, NX, send, 0)

        @pl.when(g >= 4)
        def _():
            ev_a2(far_first(g - 4, NZ))

        return carry

    lax.fori_loop(0, NZ, group, 0)
    wts_copy.start()
    lag_copy.start()
    finish(NZ - 1)
    ev_b2(1, 2)
    ev_b2(1, 1)
    ev_b2(1, 3)
    ev_a2(6)
    ev_b2(1, 0)
    ev_a2(1)
    ev_b2(2, 2)
    ev_ra2(4)
    ev_b2(2, 1)
    ev_ra2(3)
    ev_b2(2, 3)
    ev_b2(2, 0)
    ev_ra2(5)
    ev_rb2(2)
    ev_a2(7)
    ev_a2(0)
    ev_ra2(2)
    ev_ra2(6)
    ev_ra2(1)
    ev_rb2(1)
    ev_rb2(3)
    ev_ra2(7)
    ev_ra2(0)
    ev_rb2(0)

    loads[2].wait()
    wts_copy.wait()
    lag_copy.wait()
    lane16 = lax.broadcasted_iota(jnp.int32, (16, 128), 1)
    cols = tuple(jnp.zeros((16, 128), jnp.float32) for _ in range(2))
    for j in range(2):
        def project(o, carry):
            d0, d1, d2 = dir_ref[o, 0], dir_ref[o, 1], dir_ref[o, 2]
            coef = [d0 * d0, d1 * d1, d2 * d2, 2.0 * d0 * d1, 2.0 * d0 * d2, 2.0 * d1 * d2]
            new = []
            for chunk in range(2):
                moment = None
                for tile, (ch, comp) in enumerate(TILES):
                    if ch == chunk:
                        term = coef[comp] * C[0, 0, place(j, tile)]
                        moment = term if moment is None else moment + term
                weight = W[j, o, pl.ds(chunk * 16, 16), :].astype(jnp.float32)
                value = jnp.sum(weight * moment, axis=1, keepdims=True)
                new.append(jnp.where(lane16 == j * 64 + o, value, carry[chunk]))
            return tuple(new)

        cols = lax.fori_loop(0, 64, project, cols, unroll=4)

    mine = yy * 2 + c
    G[mine, pl.ds(0, 16), :] = cols[0]
    G[mine, pl.ds(16, 16), :] = cols[1]
    for dy in range(NY):
        for dc in range(2):
            if dy or dc:
                remote(
                    G.at[mine], G.at[mine], sg, rg, chip * 2 + (c + dc) % 2, (yy + dy) % NY
                ).start()
    gathered = remote(G.at[pl.ds(0, 7)], G.at[pl.ds(0, 7)], sg, rg, mate)
    gathered.wait_send()
    gathered.wait_recv()

    period = G[...].reshape(256, 128)
    curved = pltpu.roll(period, 255, 0) - 2.0 * period + pltpu.roll(period, 1, 0)
    lane = lax.broadcasted_iota(jnp.int32, (8, 128), 1)
    lags = jnp.where(lane // 64 == c, lag_ref[...], lag2[...])
    lags = ((lags + 256 - yy * 64) % 256)[0:1, :]
    shifted = curved
    for bit in range(8):
        chosen = jnp.broadcast_to((lags // (1 << bit)) % 2 == 1, (256, 128))
        shifted = jnp.where(chosen, pltpu.roll(shifted, 1 << bit, 0), shifted)
    slab = shifted[0:64, :]
    slab = slab + pltpu.roll(slab, 64, 1)
    M[...] = jnp.transpose(jnp.concatenate([slab, slab], axis=0))
    for i in range(32):
        HS[i] = M[pl.ds(2 * i + c, 1), :]

    def m_h(r):
        to = dev(r // NZ, r % NZ, c)
        return remote(HS.at[to // 2], HR.at[r - 1], sh, rh, to)

    def send(r, carry):
        m_h(r).start()
        return carry

    lax.fori_loop(1, 32, send, 0)

    wait_all = [core_copy(i, j) for i in range(NX) for j in range(NZ)]
    wait_all += [m_a1(d, j) for d in range(2) for j in range(NZ)]
    wait_all += [m_a2(d, j) for d in range(2) for j in range(NZ)]
    wait_all += [m_a3(d) for d in range(2)]
    wait_all += [m_a4(d, k) for d in range(2) for k in range(3)]
    wait_all += [m_b1(d, i) for d in range(2) for i in range(NX)]
    wait_all += [m_b2(d, k, i) for d in range(2) for k in range(3) for i in range(NX)]
    wait_all += [m_b3(d) for d in range(2)]
    wait_all += [m_b4(d) for d in range(2)]
    for copy in wait_all:
        copy.wait_send()

    own = HS[chip]
    scattered = remote(HS.at[pl.ds(0, 31)], HR.at[pl.ds(0, 31)], sh, rh, mate)
    scattered.wait_send()
    scattered.wait_recv()
    total = own + jnp.sum(HR[...], axis=0)
    out_ref[...] = total[:, 0:64]


def body(density, flow_rest, dest, weights, directions, bins):
    lists, lags = pl.pallas_call(
        prep_kernel,
        out_shape=(
            jax.ShapeDtypeStruct((8, 128), jnp.int32),
            jax.ShapeDtypeStruct((8, 128), jnp.int32),
        ),
        name="prep",
    )(dest, bins)
    f32, bf16 = jnp.float32, jnp.bfloat16
    vm, dma = pltpu.VMEM, pltpu.SemaphoreType.DMA
    tile = (16, 128)
    scratch = [
        vm((ROWS_DEV + 1, 64, 128), bf16),
        vm((ROWS_DEV + 1, 4, 64, 128), bf16),
        vm((NX, NZ, 24) + tile, f32),
        vm((NX, NZ, 24) + tile, f32),
        vm((NX, NZ, 24) + tile, f32),
        vm((2, NZ, NA) + tile, f32),
        vm((2, NZ, 2 * NA) + tile, f32),
        vm((2, NA) + tile, f32),
        vm((2, 3, 2 * NA) + tile, f32),
        vm((2, NX, NB) + tile, f32),
        vm((2, 3, NX, 2 * NB) + tile, f32),
        vm((2, NB) + tile, f32),
        vm((2, 2 * NB) + tile, f32),
        vm((2, 64, 32, 128), bf16),
        vm((8, 128), jnp.int32),
        vm((8, 32, 128), f32),
        vm((128, 128), f32),
        vm((32, 1, 128), f32),
        vm((31, 1, 128), f32),
        dma((3,)),
    ]
    for shape in ((NX, NZ), (2, NZ), (2, NZ), (2,), (2, 3), (2, NX), (2, 3, NX), (2,), (2,)):
        scratch += [dma(shape), dma(shape)]
    scratch += [dma(())] * 8
    return pl.pallas_call(
        main_kernel,
        out_shape=jax.ShapeDtypeStruct((1, 64), f32),
        in_specs=[
            pl.BlockSpec(memory_space=pltpu.SMEM),
            pl.BlockSpec(memory_space=pltpu.SMEM),
            pl.BlockSpec(memory_space=pltpu.VMEM),
            pl.BlockSpec(memory_space=pl.ANY),
            pl.BlockSpec(memory_space=pl.ANY),
            pl.BlockSpec(memory_space=pl.ANY),
        ],
        out_specs=pl.BlockSpec(memory_space=pltpu.VMEM),
        scratch_shapes=scratch,
        compiler_params=pltpu.CompilerParams(
            collective_id=0, has_side_effects=True, vmem_limit_bytes=60 << 20
        ),
        name="rotor",
    )(lists, directions, lags, density, flow_rest, weights)


def solution(mesh):
    placed = (
        P("blk", "tm", None),
        P("blk", None, "tm", None),
        P("blk", None),
        P("blk", None, "tm", None),
        P(),
        P(None, "blk"),
    )
    return jax.shard_map(
        body, mesh=mesh, in_specs=placed, out_specs=P("blk", "tm"), check_vma=False
    )
```

time: 804 us -> 78.5 us (0.10)
  waiting for transfers between devices: 422 us -> 0 us
  blocking collectives: 253 us -> 0 us
  local copies, waits for them, and re-layouts: 88.2 us -> 5.28 us
  Pallas kernels: 0 us -> 73 us
  starting transfers between devices: 19.1 us -> 0 us
  other arithmetic: 13.4 us -> 0 us
    all_to_all x2 -> x0, waiting for transfers between devices: 422 us -> none  [the longest x1 365 us: body(): lax.all_to_all(send_flow, 'blk', split_axis=0, concat_axis=0, tiled=True)]
    unnamed x1 -> x0, blocking collectives: 243 us -> none
    pallas_call x0 -> x2, Pallas kernels: none -> 73 us  [the longest x1 71.3 us: body(): pl.pallas_call(main_kernel, out_shape=jax.ShapeDtypeStruct((1, 64), f32),...]
    gather x3 -> x0, local copies, waits for them, and re-layouts: 32.9 us -> none  [body(): shifted = jnp.take_along_axis(curved, lagged, axis=1)]
    scatter x2 -> x0, local copies, waits for them, and re-layouts: 29.6 us -> none  [the longest x1 17.7 us: body(): jnp.zeros((blocks * capacity, 4, slab_len, cells), jnp.bfloat16)]
    all_to_all x2 -> x0, starting transfers between devices: 19.1 us -> none  [the longest x1 13.1 us: body(): lax.all_to_all(send_dens, 'blk', split_axis=0, concat_axis=0, tiled=True)]
    reshape x1 -> x0, local copies, waits for them, and re-layouts: 14.1 us -> none  [body(): send_flow = send_flow.reshape(blocks, capacity, 4, slab_len, cells)]
    reduce_sum x3 -> x0, other arithmetic: 11.4 us -> none  [the longest x1 10.5 us: stress_terms(): pieces = [jnp.sum(term, axis=0) for term in pieces]]
  transfers between devices with their start and end apart: 2 -> 0, of which waited for: 2 -> 0; matrix products, arithmetic and copies ran while one was open for 5% -> 0% of each run, Pallas kernels for 0% -> 0%
where the time goes in v1:
time: 78.5 us; the launch traced here: 78.2 us
  Pallas kernels  73 us (93%)
  local copies, waits for them, and re-layouts  5.28 us (7%)
    pallas_call x1, Pallas kernels, body(): pl.pallas_call(main_kernel, out_shape=jax.ShapeDtypeStruct((1, 64), f32),...  71.3 us
    unnamed x4, local copies, waits for them, and re-layouts  5.28 us
    pallas_call x1, Pallas kernels, body(): pl.pallas_call(prep_kernel, out_shape=(jax.ShapeDtypeStruct((8, 128), jnp...  1.68 us

profile of v1, /device:TPU:1, one launch (start us, length us, event | category | flops | bytes accessed | tf_op | source)
XLA Modules:
  0.0 78.2 jit_solution(10289000684387693156)
XLA Ops:
  0.0 1.4 %copy.7.dest_ref = s32[96,1]{1,0:T(8,128)} copy(s32[96,1]{0,1:T(1,128)} %param.8) | data formatting | bytes 768 | tf_op args[2]
  1.4 1.3 %copy.8.bins_ref = s32[64,1]{1,0:T(8,128)} copy(s32[64,1]{0,1:T(1,128)} %param.11) | data formatting | bytes 512 | tf_op args[5]
  2.7 1.7 %prep.1 = (s32[8,128]{1,0:T(8,128)}, s32[8,128]{1,0:T(8,128)}) custom-call(s32[96,1]{1,0:T(8,128)} %copy.7.dest_ref, s32[64,1]{1,0:T(8,128)} %copy.8.bins_ref), custom_call_target="tpu_custom_call" | custom-call | tf_op jit(solution)/shard_map/prep/pallas_call | solution.py:392
  4.4 1.4 %copy.9.dir_ref = f32[64,3]{1,0:T(8,128)} copy(f32[64,3]{0,1:T(4,128)} %param.10) | data formatting | bytes 1536 | tf_op args[4]
  5.8 71.3 %rotor.1 = f32[1,64]{1,0:T(1,128)} custom-call(s32[8,128]{1,0:T(8,128)} %get-tuple-element.7.list_ref, f32[64,3]{1,0:T(8,128)} %copy.9.dir_ref, s32[8,128]{1,0:T(8,128)} %get-tuple-element.8.lag_ref, bf16[96,64,128]{2,1,0:T(8,128)(2,1)} %dens_hbm.1, bf16[96,4,64,128]{3,2,1,0:T(8,128)(2,1)} %flow_hbm.1, bf16[1,64,64,128]{3,2,1,0:T(8,128)(2,1)} %wts_hbm.1), custom_call_target="tpu_custom_call" | custom-call | tf_op jit(solution)/shard_map/rotor/pallas_call | solution.py:428
  77.1 1.2 %copy.11 = f32[1,64]{1,0:T(1,128)} copy(f32[1,64]{1,0:T(1,128)} %rotor.1) | data formatting | bytes 512

commit v2 on v1

--- a/solution.py
+++ b/solution.py
@@ -1,5 +1,3 @@
-import functools
-
 import jax
 import jax.numpy as jnp
 from jax import lax
@@ -29,33 +27,11 @@
     return (n // 2 + step * (1 - 2 * (i % 2))) % n
 
 
-def prep_kernel(dest_ref, bins_ref, list_ref, lag_ref):
-    dest = jnp.broadcast_to(dest_ref[...], (ROWS_DEV, 128))
-    lane = lax.broadcasted_iota(jnp.int32, (ROWS_DEV, 128), 1)
-    row = lax.broadcasted_iota(jnp.int32, (ROWS_DEV, 128), 0)
-    hit = dest == lane
-    earlier = (
-        lax.broadcasted_iota(jnp.int32, (ROWS_DEV, ROWS_DEV), 0)
-        > lax.broadcasted_iota(jnp.int32, (ROWS_DEV, ROWS_DEV), 1)
-    ).astype(jnp.bfloat16)
-    before = jnp.dot(
-        earlier, hit.astype(jnp.bfloat16), preferred_element_type=jnp.float32
-    ).astype(jnp.int32)
-    for s in range(8):
-        chosen = jnp.where(hit & (before == s), row, ROWS_DEV)
-        list_ref[pl.ds(s, 1), :] = jnp.min(chosen, axis=0, keepdims=True)
-    bins = jnp.broadcast_to(bins_ref[...], (64, 128))
-    lane64 = lax.broadcasted_iota(jnp.int32, (64, 128), 1) % 64
-    row64 = lax.broadcasted_iota(jnp.int32, (64, 128), 0)
-    lags = jnp.sum(jnp.where(lane64 == row64, bins, 0), axis=0, keepdims=True)
-    lag_ref[...] = jnp.broadcast_to(lags, (8, 128))
-
-
 def main_kernel(
-    list_ref, dir_ref, lag_ref, dens_hbm, flow_hbm, wts_hbm, out_ref,
-    dens, flow, C, S, R0, RA1, RA2, RA3, RA4, RB1, RB2, RB3, RB4, W, lag2, G, M, HS, HR,
+    dir_ref, dest_ref, bins_ref, dens_hbm, flow_hbm, wts_hbm, out_ref,
+    dens, flow, list_vm, list_ref, lag_ref, C, S, R0, RA1, RA2, RA3, RA4, RB1, RB2, RB3, RB4, W, lag2, Z, G, M, HS, HR,
     ld_sem, s0, r0, sa1, ra1, sa2, ra2, sa3, ra3, sa4, ra4,
-    sb1, rb1, sb2, rb2, sb3, rb3, sb4, rb4, sw, rw, sl, rl, sg, rg, sh, rh,
+    sb1, rb1, sb2, rb2, sb3, rb3, sb4, rb4, sw, rw, sl, rl, sg, rg, sh, rh, met_y, met_mate,
 ):
     blk = lax.axis_index("blk")
     yy = lax.axis_index("tm")
@@ -88,22 +64,58 @@
         copy.start()
 
     barrier = pltpu.get_barrier_semaphore()
+    along_y = ((yy + 1) % NY, (yy + NY - 1) % NY)
     for to in near_x + near_z + (mate,):
         pl.semaphore_signal(barrier, inc=1, device_id=(to, yy), device_id_type=MESH)
-    for dy in range(1, NY):
-        for core in range(2):
-            pl.semaphore_signal(
-                barrier, inc=1, device_id=(chip * 2 + core, (yy + dy) % NY), device_id_type=MESH
-            )
-    pl.semaphore_wait(barrier, 5 + 2 * (NY - 1))
+    for to in along_y:
+        pl.semaphore_signal(barrier, inc=1, device_id=(blk, to), device_id_type=MESH)
+
+    target = jnp.broadcast_to(dest_ref[...], (64, ROWS_DEV))
+    row = lax.broadcasted_iota(jnp.int32, (64, ROWS_DEV), 1)
+    hit = target == lax.broadcasted_iota(jnp.int32, (64, ROWS_DEV), 0)
+    earlier = lax.broadcasted_iota(jnp.int32, (ROWS_DEV, ROWS_DEV), 0) < lax.broadcasted_iota(
+        jnp.int32, (ROWS_DEV, ROWS_DEV), 1
+    )
+    before = jnp.dot(
+        hit.astype(jnp.float32).astype(jnp.bfloat16),
+        earlier.astype(jnp.float32).astype(jnp.bfloat16),
+        preferred_element_type=jnp.float32,
+    ).astype(jnp.int32)
+    lane64 = lax.broadcasted_iota(jnp.int32, (64, 128), 1)
+    lists = jnp.full((64, 128), ROWS_DEV, jnp.int32)
+    for s in range(SLOTS):
+        chosen = jnp.min(
+            jnp.where(hit & (before == s), row, ROWS_DEV), axis=1, keepdims=True
+        )
+        lists = jnp.where(lane64 == s, chosen, lists)
+    list_vm[...] = lists
+    list_copy = pltpu.make_async_copy(list_vm, list_ref, ld_sem.at[3])
+    list_copy.start()
+
+    source = lax.broadcasted_iota(jnp.int32, (64, 128), 0)
+    wanted = 2 * (lane64 % 32) + lane64 // 64
+    spread = jnp.where(
+        source == wanted, 1.0, 0.0
+    )
+    lag_ref[...] = jnp.dot(
+        jnp.broadcast_to(bins_ref[...], (8, 64)).astype(jnp.float32).astype(jnp.bfloat16),
+        spread.astype(jnp.bfloat16),
+        preferred_element_type=jnp.float32,
+    ).astype(jnp.int32)
+
+    dens[ROWS_DEV] = jnp.zeros((64, 128), jnp.bfloat16)
+    flow[ROWS_DEV] = jnp.zeros((4, 64, 128), jnp.bfloat16)
+
+    pl.semaphore_wait(barrier, 7)
+    for to in along_y:
+        pl.semaphore_signal(met_y, inc=1, device_id=(blk, to), device_id_type=MESH)
 
     wts_copy = remote(
         wts_hbm.at[0, :, pl.ds(pl.multiple_of((1 - c) * 32, 32), 32), :], W.at[c], sw, rw, mate
     )
     lag_copy = remote(lag_ref, lag2, sl, rl, mate)
 
-    dens[ROWS_DEV] = jnp.zeros((64, 128), jnp.bfloat16)
-    flow[ROWS_DEV] = jnp.zeros((4, 64, 128), jnp.bfloat16)
+    list_copy.wait()
     loads[0].wait()
     loads[1].wait()
 
@@ -113,7 +125,7 @@
     def unit(dx, dz):
         first = dev(dx, dz, 0)
         for j in range(2):
-            rows = [list_ref[s, first + j] for s in range(SLOTS)]
+            rows = [list_ref[first + j, s] for s in range(SLOTS)]
             for part in range(2):
                 target = C if part == 0 else S
                 for chunk in range(2):
@@ -281,6 +293,8 @@
     lax.fori_loop(0, NZ, group, 0)
     wts_copy.start()
     lag_copy.start()
+    pl.semaphore_wait(met_y, 2)
+    pl.semaphore_signal(met_mate, inc=1, device_id=(mate, yy), device_id_type=MESH)
     finish(NZ - 1)
     ev_b2(1, 2)
     ev_b2(1, 1)
@@ -311,13 +325,14 @@
     wts_copy.wait()
     lag_copy.wait()
     lane16 = lax.broadcasted_iota(jnp.int32, (16, 128), 1)
-    cols = tuple(jnp.zeros((16, 128), jnp.float32) for _ in range(2))
-    for j in range(2):
-        def project(o, carry):
-            d0, d1, d2 = dir_ref[o, 0], dir_ref[o, 1], dir_ref[o, 2]
-            coef = [d0 * d0, d1 * d1, d2 * d2, 2.0 * d0 * d1, 2.0 * d0 * d2, 2.0 * d1 * d2]
-            new = []
-            for chunk in range(2):
+
+    def project(o, carry):
+        d0, d1, d2 = dir_ref[0, o], dir_ref[1, o], dir_ref[2, o]
+        coef = [d0 * d0, d1 * d1, d2 * d2, 2.0 * d0 * d1, 2.0 * d0 * d2, 2.0 * d1 * d2]
+        new = []
+        for chunk in range(2):
+            out = carry[chunk]
+            for j in range(2):
                 moment = None
                 for tile, (ch, comp) in enumerate(TILES):
                     if ch == chunk:
@@ -325,38 +340,44 @@
                         moment = term if moment is None else moment + term
                 weight = W[j, o, pl.ds(chunk * 16, 16), :].astype(jnp.float32)
                 value = jnp.sum(weight * moment, axis=1, keepdims=True)
-                new.append(jnp.where(lane16 == j * 64 + o, value, carry[chunk]))
-            return tuple(new)
-
-        cols = lax.fori_loop(0, 64, project, cols, unroll=4)
-
+                out = jnp.where(lane16 == (o % 2) * 64 + j * 32 + o // 2, value, out)
+            new.append(out)
+        return tuple(new)
+
+    zero = jnp.zeros((16, 128), jnp.float32)
+    cols = lax.fori_loop(0, 64, project, (zero, zero), unroll=2)
+
+    low = lane16 < 64
+    Z[0] = jnp.where(low, cols[0], pltpu.roll(cols[1], 64, 1))
+    Z[1] = jnp.where(low, pltpu.roll(cols[0], 64, 1), cols[1])
+    pl.semaphore_wait(met_mate, 1)
     mine = yy * 2 + c
-    G[mine, pl.ds(0, 16), :] = cols[0]
-    G[mine, pl.ds(16, 16), :] = cols[1]
-    for dy in range(NY):
-        for dc in range(2):
+    for dc in range(2):
+        for dy in range(NY):
+            core = (c + dc) % 2
             if dy or dc:
-                remote(
-                    G.at[mine], G.at[mine], sg, rg, chip * 2 + (c + dc) % 2, (yy + dy) % NY
-                ).start()
+                remote(Z.at[core], G.at[mine], sg, rg, chip * 2 + core, (yy + dy) % NY).start()
+    G[mine] = Z[c]
     gathered = remote(G.at[pl.ds(0, 7)], G.at[pl.ds(0, 7)], sg, rg, mate)
-    gathered.wait_send()
     gathered.wait_recv()
 
-    period = G[...].reshape(256, 128)
+    held = G[...]
+    period = jnp.concatenate([held, pltpu.roll(held, 64, 2)], axis=1).reshape(256, 128)
     curved = pltpu.roll(period, 255, 0) - 2.0 * period + pltpu.roll(period, 1, 0)
     lane = lax.broadcasted_iota(jnp.int32, (8, 128), 1)
-    lags = jnp.where(lane // 64 == c, lag_ref[...], lag2[...])
+    own_half = jnp.where((lane // 32) % 2 == c, lag_ref[...], lag2[...])
+    lags = jnp.where(lane // 64 == c, own_half, 0)
+    lags = lags + pltpu.roll(lags, 64, 1)
     lags = ((lags + 256 - yy * 64) % 256)[0:1, :]
     shifted = curved
     for bit in range(8):
         chosen = jnp.broadcast_to((lags // (1 << bit)) % 2 == 1, (256, 128))
         shifted = jnp.where(chosen, pltpu.roll(shifted, 1 << bit, 0), shifted)
     slab = shifted[0:64, :]
-    slab = slab + pltpu.roll(slab, 64, 1)
+    slab = slab + pltpu.roll(slab, 96, 1)
     M[...] = jnp.transpose(jnp.concatenate([slab, slab], axis=0))
     for i in range(32):
-        HS[i] = M[pl.ds(2 * i + c, 1), :]
+        HS[i] = M[pl.ds(i, 1), :]
 
     def m_h(r):
         to = dev(r // NZ, r % NZ, c)
@@ -377,6 +398,7 @@
     wait_all += [m_b2(d, k, i) for d in range(2) for k in range(3) for i in range(NX)]
     wait_all += [m_b3(d) for d in range(2)]
     wait_all += [m_b4(d) for d in range(2)]
+    gathered.wait_send()
     for copy in wait_all:
         copy.wait_send()
 
@@ -389,20 +411,15 @@
 
 
 def body(density, flow_rest, dest, weights, directions, bins):
-    lists, lags = pl.pallas_call(
-        prep_kernel,
-        out_shape=(
-            jax.ShapeDtypeStruct((8, 128), jnp.int32),
-            jax.ShapeDtypeStruct((8, 128), jnp.int32),
-        ),
-        name="prep",
-    )(dest, bins)
     f32, bf16 = jnp.float32, jnp.bfloat16
     vm, dma = pltpu.VMEM, pltpu.SemaphoreType.DMA
     tile = (16, 128)
     scratch = [
         vm((ROWS_DEV + 1, 64, 128), bf16),
         vm((ROWS_DEV + 1, 4, 64, 128), bf16),
+        vm((64, 128), jnp.int32),
+        pltpu.SMEM((64, 128), jnp.int32),
+        vm((8, 128), jnp.int32),
         vm((NX, NZ, 24) + tile, f32),
         vm((NX, NZ, 24) + tile, f32),
         vm((NX, NZ, 24) + tile, f32),
@@ -416,21 +433,22 @@
         vm((2, 2 * NB) + tile, f32),
         vm((2, 64, 32, 128), bf16),
         vm((8, 128), jnp.int32),
-        vm((8, 32, 128), f32),
+        vm((2,) + tile, f32),
+        vm((8,) + tile, f32),
         vm((128, 128), f32),
         vm((32, 1, 128), f32),
         vm((31, 1, 128), f32),
-        dma((3,)),
+        dma((4,)),
     ]
     for shape in ((NX, NZ), (2, NZ), (2, NZ), (2,), (2, 3), (2, NX), (2, 3, NX), (2,), (2,)):
         scratch += [dma(shape), dma(shape)]
-    scratch += [dma(())] * 8
+    scratch += [dma(())] * 8 + [pltpu.SemaphoreType.REGULAR] * 2
     return pl.pallas_call(
         main_kernel,
         out_shape=jax.ShapeDtypeStruct((1, 64), f32),
         in_specs=[
             pl.BlockSpec(memory_space=pltpu.SMEM),
-            pl.BlockSpec(memory_space=pltpu.SMEM),
+            pl.BlockSpec(memory_space=pltpu.VMEM),
             pl.BlockSpec(memory_space=pltpu.VMEM),
             pl.BlockSpec(memory_space=pl.ANY),
             pl.BlockSpec(memory_space=pl.ANY),
@@ -442,7 +460,7 @@
             collective_id=0, has_side_effects=True, vmem_limit_bytes=60 << 20
         ),
         name="rotor",
-    )(lists, directions, lags, density, flow_rest, weights)
+    )(directions.T, dest.T, bins.T, density, flow_rest, weights)
 
 
 def solution(mesh):

time: 78.5 us -> 71.7 us (0.913)
  local copies, waits for them, and re-layouts: 5.28 us -> 1.19 us
  Pallas kernels: 73 us -> 70.4 us
    unnamed x4 -> x1, local copies, waits for them, and re-layouts: 5.28 us -> 1.19 us
    pallas_call x1 -> x0, Pallas kernels: 1.68 us -> none  [body(): pl.pallas_call(prep_kernel, out_shape=(jax.ShapeDtypeStruct((8, 128), jnp...]
    pallas_call x1, Pallas kernels: 71.3 us -> 70.4 us  [body(): pl.pallas_call(main_kernel, out_shape=jax.ShapeDtypeStruct((1, 64), f32),...]
where the time goes in v2:
time: 71.7 us; the launch traced here: 71.6 us
  Pallas kernels  70.4 us (98%)
  local copies, waits for them, and re-layouts  1.19 us (2%)
    pallas_call x1, Pallas kernels, body(): pl.pallas_call(main_kernel, out_shape=jax.ShapeDtypeStruct((1, 64), f32),...  70.4 us

profile of v2, /device:TPU:1, one launch (start us, length us, event | category | flops | bytes accessed | tf_op | source)
XLA Modules:
  0.0 71.6 jit_solution(11418191286375087983)
XLA Ops:
  0.0 70.4 %rotor.1 = f32[1,64]{1,0:T(1,128)} custom-call(f32[3,64]{1,0:T(4,128)} %bitcast.3, s32[1,96]{1,0:T(1,128)} %bitcast.4, s32[1,64]{1,0:T(1,128)} %bitcast.5, bf16[96,64,128]{2,1,0:T(8,128)(2,1)} %dens_hbm.1, bf16[96,4,64,128]{3,2,1,0:T(8,128)(2,1)} %flow_hbm.1, bf16[1,64,64,128]{3,2,1,0:T(8,128)(2,1)} %wts_hbm.1), custom_call_target="tpu_custom_call" | custom-call | tf_op jit(solution)/shard_map/rotor/pallas_call | solution.py:446
  70.4 1.2 %copy.8 = f32[1,64]{1,0:T(1,128)} copy(f32[1,64]{1,0:T(1,128)} %rotor.1) | data formatting | bytes 512

commit v3 on v2

--- a/solution.py
+++ b/solution.py
@@ -8,12 +8,13 @@
 NX, NZ, NY = 4, 8, 4
 ROWS_DEV = 96
 SLOTS = 4
-NA = 7
+NA = 8
 NB = 12 - NA
 TILES = [(0, i) for i in range(6)] + [(1, i) for i in (5, 4, 3, 2, 1, 0)]
 A0, A1, A2 = 0, NA, 2 * NA
 B0, B1, B2 = 2 * NA, 2 * NA + NB, 2 * NA + 2 * NB
 MESH = pl.DeviceIdType.MESH
+STEPS = 32512.0
 
 
 def place(j, tile):
@@ -27,9 +28,29 @@
     return (n // 2 + step * (1 - 2 * (i % 2))) % n
 
 
+def encode(x0, x1):
+    parts, steps = [], []
+    for x in (x0, x1):
+        hi = x.astype(jnp.bfloat16)
+        wide = hi.astype(jnp.float32)
+        ratio = (x - wide) / jnp.where(wide == 0.0, 1.0, wide)
+        parts.append(hi)
+        steps.append((ratio * STEPS + 128.5).astype(jnp.int32))
+    return parts[0], parts[1], ((steps[0] - 128) * 256 + steps[1]).astype(jnp.int16)
+
+
+def decode(hi0, hi1, low):
+    low = low.astype(jnp.int32)
+    out = []
+    for hi, step in ((hi0, low >> 8), (hi1, (low & 255) - 128)):
+        out.append(hi.astype(jnp.float32) * (1.0 + step.astype(jnp.float32) * (1.0 / STEPS)))
+    return out
+
+
 def main_kernel(
-    dir_ref, dest_ref, bins_ref, dens_hbm, flow_hbm, wts_hbm, out_ref,
-    dens, flow, list_vm, list_ref, lag_ref, C, S, R0, RA1, RA2, RA3, RA4, RB1, RB2, RB3, RB4, W, lag2, Z, G, M, HS, HR,
+    dir_hbm, dest_hbm, bins_hbm, dens_hbm, flow_hbm, wts_hbm, out_ref,
+    dir_ref, dest_ref, bins_ref, dens, flow, list_vm, list_ref, lag_ref, C, S, R0, HC, LC, RA1, LA1, RA2, LA2, RA3, LA3, RA4, LA4,
+    RB1, LB1, RB2, LB2, RB3, LB3, RB4, LB4, W, lag2, Z, G, M, HS, HR,
     ld_sem, s0, r0, sa1, ra1, sa2, ra2, sa3, ra3, sa4, ra4,
     sb1, rb1, sb2, rb2, sb3, rb3, sb4, rb4, sw, rw, sl, rl, sg, rg, sh, rh, met_y, met_mate,
 ):
@@ -53,6 +74,18 @@
             device_id=(to, yy if ty is None else ty), device_id_type=MESH,
         )
 
+    barrier = pltpu.get_barrier_semaphore()
+    along_y = ((yy + 1) % NY, (yy + NY - 1) % NY)
+    for to in near_x + near_z + (mate,):
+        pl.semaphore_signal(barrier, inc=1, device_id=(to, yy), device_id_type=MESH)
+    for to in along_y:
+        pl.semaphore_signal(barrier, inc=1, device_id=(blk, to), device_id_type=MESH)
+
+    small = [
+        pltpu.make_async_copy(dest_hbm, dest_ref, ld_sem.at[4]),
+        pltpu.make_async_copy(bins_hbm, bins_ref, ld_sem.at[5]),
+        pltpu.make_async_copy(dir_hbm, dir_ref, ld_sem.at[6]),
+    ]
     loads = [
         pltpu.make_async_copy(dens_hbm, dens.at[pl.ds(0, ROWS_DEV)], ld_sem.at[0]),
         pltpu.make_async_copy(flow_hbm, flow.at[pl.ds(0, ROWS_DEV)], ld_sem.at[1]),
@@ -60,46 +93,41 @@
             wts_hbm.at[0, :, pl.ds(pl.multiple_of(c * 32, 32), 32), :], W.at[c], ld_sem.at[2]
         ),
     ]
-    for copy in loads:
+    for copy in small + loads:
         copy.start()
-
-    barrier = pltpu.get_barrier_semaphore()
-    along_y = ((yy + 1) % NY, (yy + NY - 1) % NY)
-    for to in near_x + near_z + (mate,):
-        pl.semaphore_signal(barrier, inc=1, device_id=(to, yy), device_id_type=MESH)
-    for to in along_y:
-        pl.semaphore_signal(barrier, inc=1, device_id=(blk, to), device_id_type=MESH)
+    small[0].wait()
+    small[1].wait()
 
     target = jnp.broadcast_to(dest_ref[...], (64, ROWS_DEV))
-    row = lax.broadcasted_iota(jnp.int32, (64, ROWS_DEV), 1)
     hit = target == lax.broadcasted_iota(jnp.int32, (64, ROWS_DEV), 0)
     earlier = lax.broadcasted_iota(jnp.int32, (ROWS_DEV, ROWS_DEV), 0) < lax.broadcasted_iota(
         jnp.int32, (ROWS_DEV, ROWS_DEV), 1
     )
-    before = jnp.dot(
-        hit.astype(jnp.float32).astype(jnp.bfloat16),
-        earlier.astype(jnp.float32).astype(jnp.bfloat16),
-        preferred_element_type=jnp.float32,
-    ).astype(jnp.int32)
+
+    def exact(flags):
+        return jnp.where(flags, 1.0, 0.0).astype(jnp.bfloat16)
+
+    before = jnp.dot(exact(hit), exact(earlier), preferred_element_type=jnp.float32)
+    lane96 = lax.broadcasted_iota(jnp.int32, (ROWS_DEV, 128), 1)
+    number = lax.broadcasted_iota(jnp.int32, (ROWS_DEV, 128), 0) - ROWS_DEV
+    lists = jnp.full((64, 128), float(ROWS_DEV), jnp.float32)
+    for s in range(SLOTS):
+        column = jnp.where(lane96 == s, number, 0).astype(jnp.float32).astype(jnp.bfloat16)
+        lists = lists + jnp.dot(
+            exact(hit & (before == float(s))), column, preferred_element_type=jnp.float32
+        )
+    lists = jnp.clip(lists.astype(jnp.int32), 0, ROWS_DEV)
     lane64 = lax.broadcasted_iota(jnp.int32, (64, 128), 1)
-    lists = jnp.full((64, 128), ROWS_DEV, jnp.int32)
-    for s in range(SLOTS):
-        chosen = jnp.min(
-            jnp.where(hit & (before == s), row, ROWS_DEV), axis=1, keepdims=True
-        )
-        lists = jnp.where(lane64 == s, chosen, lists)
     list_vm[...] = lists
     list_copy = pltpu.make_async_copy(list_vm, list_ref, ld_sem.at[3])
     list_copy.start()
 
     source = lax.broadcasted_iota(jnp.int32, (64, 128), 0)
     wanted = 2 * (lane64 % 32) + lane64 // 64
-    spread = jnp.where(
-        source == wanted, 1.0, 0.0
-    )
+    spread = exact(source == wanted)
     lag_ref[...] = jnp.dot(
         jnp.broadcast_to(bins_ref[...], (8, 64)).astype(jnp.float32).astype(jnp.bfloat16),
-        spread.astype(jnp.bfloat16),
+        spread,
         preferred_element_type=jnp.float32,
     ).astype(jnp.int32)
 
@@ -147,44 +175,87 @@
                             target[dx, dz, place(j, tile)] = sums[comp]
         core_copy(dx, dz).start()
 
-    def add(dx, dz, lo, hi, *others):
-        span = pl.ds(lo, hi - lo)
-        total = C[dx, dz, span]
-        for ref in others:
-            total = total + ref[...]
-        C[dx, dz, span] = total
+    def combine(dx, dz, spans, send):
+        for lo, hi, came in spans:
+
+            def pair(p, carry):
+                t = lo + 2 * p
+                sums = [C[dx, dz, t], C[dx, dz, t + 1]]
+                for hi_ref, low_ref, start in came:
+                    k = t - start
+                    more = decode(hi_ref[k], hi_ref[k + 1], low_ref[(lo - start) // 2 + p])
+                    sums = [q + r for q, r in zip(sums, more)]
+                if send:
+                    h0, h1, low = encode(*sums)
+                    HC[dx, dz, t] = h0
+                    HC[dx, dz, t + 1] = h1
+                    LC[dx, dz, lo // 2 + p] = low
+                else:
+                    C[dx, dz, t] = sums[0]
+                    C[dx, dz, t + 1] = sums[1]
+                return carry
+
+            lax.fori_loop(0, (hi - lo) // 2, pair, 0, unroll=4)
 
     half_a = ((A0, A1), (A1, A2))
     half_b = ((B0, B1), (B1, B2))
 
-    def src(dx, dz, lo, hi):
-        return C.at[dx, dz, pl.ds(lo, hi - lo)]
+    class Message:
+        def __init__(self, dx, dz, span, hi_ref, low_ref, ssem, rsem, to):
+            lo, n = span[0], span[1] - span[0]
+            self.copies = [
+                remote(HC.at[dx, dz, pl.ds(lo, n)], hi_ref, ssem(0), rsem(0), to),
+                remote(LC.at[dx, dz, pl.ds(lo // 2, n // 2)], low_ref, ssem(1), rsem(1), to),
+            ]
+            self.came = (hi_ref, low_ref, lo)
+
+        def start(self):
+            for copy in self.copies:
+                copy.start()
+
+        def wait_send(self):
+            for copy in self.copies:
+                copy.wait_send()
+
+        def wait_recv(self):
+            for copy in self.copies:
+                copy.wait_recv()
+            return self.came
+
+    def message(dx, dz, span, hi_ref, low_ref, ssem, rsem, to, *at):
+        return Message(
+            dx, dz, span, hi_ref.at[at], low_ref.at[at],
+            lambda i: ssem.at[at + (i,)], lambda i: rsem.at[at + (i,)], to,
+        )
 
     def m_a1(d, dz):
-        return remote(src(2, dz, *half_a[d]), RA1.at[d, dz], sa1.at[d, dz], ra1.at[d, dz], near_x[d])
+        return message(2, dz, half_a[d], RA1, LA1, sa1, ra1, near_x[d], d, dz)
 
     def m_a2(d, dz):
-        return remote(src(1 if d == 0 else 3, dz, A0, A2), RA2.at[d, dz], sa2.at[d, dz], ra2.at[d, dz], near_x[d])
+        return message(1 if d == 0 else 3, dz, (A0, A2), RA2, LA2, sa2, ra2, near_x[d], d, dz)
 
     def m_a3(d):
-        return remote(src(0, 4, *half_a[d]), RA3.at[d], sa3.at[d], ra3.at[d], near_z[d])
+        return message(0, 4, half_a[d], RA3, LA3, sa3, ra3, near_z[d], d)
 
     def m_a4(d, k):
         dz = 3 - k if d == 0 else 5 + k
-        return remote(src(0, dz, A0, A2), RA4.at[d, k], sa4.at[d, k], ra4.at[d, k], near_z[d])
+        return message(0, dz, (A0, A2), RA4, LA4, sa4, ra4, near_z[d], d, k)
 
     def m_b1(d, dx):
-        return remote(src(dx, 4, *half_b[d]), RB1.at[d, dx], sb1.at[d, dx], rb1.at[d, dx], near_z[d])
+        return message(dx, 4, half_b[d], RB1, LB1, sb1, rb1, near_z[d], d, dx)
 
     def m_b2(d, k, dx):
         dz = 3 - k if d == 0 else 5 + k
-        return remote(src(dx, dz, B0, B2), RB2.at[d, k, dx], sb2.at[d, k, dx], rb2.at[d, k, dx], near_z[d])
+        return message(dx, dz, (B0, B2), RB2, LB2, sb2, rb2, near_z[d], d, k, dx)
 
     def m_b3(d):
-        return remote(src(2, 0, *half_b[d]), RB3.at[d], sb3.at[d], rb3.at[d], near_x[d])
+        return message(2, 0, half_b[d], RB3, LB3, sb3, rb3, near_x[d], d)
 
     def m_b4(d):
-        return remote(src(1 if d == 0 else 3, 0, B0, B2), RB4.at[d], sb4.at[d], rb4.at[d], near_x[d])
+        return message(1 if d == 0 else 3, 0, (B0, B2), RB4, LB4, sb4, rb4, near_x[d], d)
+
+    def halves(pair, d, extra, both=()):
+        return [(lo, hi, list(both) + ([extra] if i == d else [])) for i, (lo, hi) in enumerate(pair)]
 
     def finish(gp):
         dz = far_first(gp, NZ)
@@ -192,17 +263,19 @@
         def step(k, carry):
             dx = far_first(k, NX)
             core_copy(dx, dz).wait_recv()
-            add(dx, dz, 0, 24, R0.at[dx, dz])
+            C[dx, dz] = C[dx, dz] + R0[dx, dz]
 
             @pl.when(k == 0)
             def _():
-                m_a1(0, dz).start()
-                m_a1(1, dz).start()
+                for d in range(2):
+                    combine(2, dz, [half_a[d] + ((),)], True)
+                    m_a1(d, dz).start()
 
             @pl.when(gp == 0)
             def _():
-                m_b1(0, dx).start()
-                m_b1(1, dx).start()
+                for d in range(2):
+                    combine(dx, 4, [half_b[d] + ((),)], True)
+                    m_b1(d, dx).start()
 
             return carry
 
@@ -210,57 +283,50 @@
 
     def ev_a2(dz):
         for d in range(2):
-            m_a1(d, dz).wait_recv()
-            add(1 if d == 0 else 3, dz, *half_a[d], RA1.at[d, dz])
+            came = m_a1(d, dz).wait_recv()
+            combine(1 if d == 0 else 3, dz, halves(half_a, d, came), True)
             m_a2(d, dz).start()
 
     def ev_b2(k, dx):
         for d in range(2):
             dz = 3 - k if d == 0 else 5 + k
             if k == 0:
-                m_b1(d, dx).wait_recv()
-                add(dx, dz, *half_b[d], RB1.at[d, dx])
+                spans = halves(half_b, d, m_b1(d, dx).wait_recv())
             else:
-                m_b2(d, k - 1, dx).wait_recv()
-                add(dx, dz, B0, B2, RB2.at[d, k - 1, dx])
+                spans = [(B0, B2, [m_b2(d, k - 1, dx).wait_recv()])]
+            combine(dx, dz, spans, True)
             m_b2(d, k, dx).start()
 
     def ev_ra2(dz):
-        m_a2(0, dz).wait_recv()
-        m_a2(1, dz).wait_recv()
-        add(0, dz, A0, A2, RA2.at[0, dz], RA2.at[1, dz])
+        both = [m_a2(0, dz).wait_recv(), m_a2(1, dz).wait_recv()]
         if dz == 4:
+            combine(0, 4, [(A0, A2, both)], True)
             m_a3(0).start()
             m_a3(1).start()
         elif dz == 0:
-            m_a4(0, 2).wait_recv()
-            m_a4(1, 2).wait_recv()
-            add(0, 0, A0, A2, RA4.at[0, 2], RA4.at[1, 2])
+            both += [m_a4(0, 2).wait_recv(), m_a4(1, 2).wait_recv()]
+            combine(0, 0, [(A0, A2, both)], False)
         else:
             d, k = (0, 3 - dz) if dz < 4 else (1, dz - 5)
             if k == 0:
-                m_a3(d).wait_recv()
-                add(0, dz, *half_a[d], RA3.at[d])
+                spans = halves(half_a, d, m_a3(d).wait_recv(), both)
             else:
-                m_a4(d, k - 1).wait_recv()
-                add(0, dz, A0, A2, RA4.at[d, k - 1])
+                spans = [(A0, A2, both + [m_a4(d, k - 1).wait_recv()])]
+            combine(0, dz, spans, True)
             m_a4(d, k).start()
 
     def ev_rb2(dx):
-        m_b2(0, 2, dx).wait_recv()
-        m_b2(1, 2, dx).wait_recv()
-        add(dx, 0, B0, B2, RB2.at[0, 2, dx], RB2.at[1, 2, dx])
+        both = [m_b2(0, 2, dx).wait_recv(), m_b2(1, 2, dx).wait_recv()]
         if dx == 2:
+            combine(2, 0, [(B0, B2, both)], True)
             m_b3(0).start()
             m_b3(1).start()
         elif dx == 0:
-            m_b4(0).wait_recv()
-            m_b4(1).wait_recv()
-            add(0, 0, B0, B2, RB4.at[0], RB4.at[1])
+            both += [m_b4(0).wait_recv(), m_b4(1).wait_recv()]
+            combine(0, 0, [(B0, B2, both)], False)
         else:
             d = 0 if dx == 1 else 1
-            m_b3(d).wait_recv()
-            add(dx, 0, *half_b[d], RB3.at[d])
+            combine(dx, 0, halves(half_b, d, m_b3(d).wait_recv(), both), True)
             m_b4(d).start()
 
     def group(g, carry):
@@ -322,6 +388,7 @@
     ev_rb2(0)
 
     loads[2].wait()
+    small[2].wait()
     wts_copy.wait()
     lag_copy.wait()
     lane16 = lax.broadcasted_iota(jnp.int32, (16, 128), 1)
@@ -345,7 +412,7 @@
         return tuple(new)
 
     zero = jnp.zeros((16, 128), jnp.float32)
-    cols = lax.fori_loop(0, 64, project, (zero, zero), unroll=2)
+    cols = lax.fori_loop(0, 64, project, (zero, zero), unroll=8)
 
     low = lane16 < 64
     Z[0] = jnp.where(low, cols[0], pltpu.roll(cols[1], 64, 1))
@@ -415,6 +482,9 @@
     vm, dma = pltpu.VMEM, pltpu.SemaphoreType.DMA
     tile = (16, 128)
     scratch = [
+        pltpu.SMEM((3, 64), f32),
+        vm((1, ROWS_DEV), jnp.int32),
+        vm((1, 64), jnp.int32),
         vm((ROWS_DEV + 1, 64, 128), bf16),
         vm((ROWS_DEV + 1, 4, 64, 128), bf16),
         vm((64, 128), jnp.int32),
@@ -423,14 +493,15 @@
         vm((NX, NZ, 24) + tile, f32),
         vm((NX, NZ, 24) + tile, f32),
         vm((NX, NZ, 24) + tile, f32),
-        vm((2, NZ, NA) + tile, f32),
-        vm((2, NZ, 2 * NA) + tile, f32),
-        vm((2, NA) + tile, f32),
-        vm((2, 3, 2 * NA) + tile, f32),
-        vm((2, NX, NB) + tile, f32),
-        vm((2, 3, NX, 2 * NB) + tile, f32),
-        vm((2, NB) + tile, f32),
-        vm((2, 2 * NB) + tile, f32),
+        vm((NX, NZ, 24) + tile, bf16),
+        vm((NX, NZ, 12) + tile, jnp.int16),
+    ]
+    for shape, n in (
+        ((2, NZ), NA), ((2, NZ), 2 * NA), ((2,), NA), ((2, 3), 2 * NA),
+        ((2, NX), NB), ((2, 3, NX), 2 * NB), ((2,), NB), ((2,), 2 * NB),
+    ):
+        scratch += [vm(shape + (n,) + tile, bf16), vm(shape + (n // 2,) + tile, jnp.int16)]
+    scratch += [
         vm((2, 64, 32, 128), bf16),
         vm((8, 128), jnp.int32),
         vm((2,) + tile, f32),
@@ -438,22 +509,18 @@
         vm((128, 128), f32),
         vm((32, 1, 128), f32),
         vm((31, 1, 128), f32),
-        dma((4,)),
+        dma((7,)),
     ]
-    for shape in ((NX, NZ), (2, NZ), (2, NZ), (2,), (2, 3), (2, NX), (2, 3, NX), (2,), (2,)):
-        scratch += [dma(shape), dma(shape)]
+    scratch += [dma((NX, NZ))] * 2
+    for shape in ((2, NZ), (2, NZ), (2,), (2, 3), (2, NX), (2, 3, NX), (2,), (2,)):
+        scratch += [dma(shape + (2,))] * 2
     scratch += [dma(())] * 8 + [pltpu.SemaphoreType.REGULAR] * 2
     return pl.pallas_call(
         main_kernel,
         out_shape=jax.ShapeDtypeStruct((1, 64), f32),
         in_specs=[
-            pl.BlockSpec(memory_space=pltpu.SMEM),
-            pl.BlockSpec(memory_space=pltpu.VMEM),
-            pl.BlockSpec(memory_space=pltpu.VMEM),
-            pl.BlockSpec(memory_space=pl.ANY),
-            pl.BlockSpec(memory_space=pl.ANY),
-            pl.BlockSpec(memory_space=pl.ANY),
-        ],
+            pl.BlockSpec(memory_space=pl.ANY)
+        ] * 6,
         out_specs=pl.BlockSpec(memory_space=pltpu.VMEM),
         scratch_shapes=scratch,
         compiler_params=pltpu.CompilerParams(

time: 71.7 us -> 63.7 us (0.89)
  Pallas kernels: 70.4 us -> 62.5 us
    pallas_call x1, Pallas kernels: 70.4 us -> 62.5 us  [body(): pl.pallas_call(main_kernel, out_shape=jax.ShapeDtypeStruct((1, 64), f32),...]
where the time goes in v3:
time: 63.7 us
  Pallas kernels  62.5 us (98%)
  local copies, waits for them, and re-layouts  1.19 us (2%)
    pallas_call x1, Pallas kernels, body(): pl.pallas_call(main_kernel, out_shape=jax.ShapeDtypeStruct((1, 64), f32),...  62.5 us

profile of v3, /device:TPU:1, one launch (start us, length us, event | category | flops | bytes accessed | tf_op | source)
XLA Modules:
  0.0 63.7 jit_solution(2905988069022926720)
XLA Ops:
  0.0 62.5 %rotor.1 = f32[1,64]{1,0:T(1,128)} custom-call(f32[3,64]{1,0:T(4,128)} %bitcast.3, s32[1,96]{1,0:T(1,128)} %bitcast.4, s32[1,64]{1,0:T(1,128)} %bitcast.5, bf16[96,64,128]{2,1,0:T(8,128)(2,1)} %dens_hbm.1, bf16[96,4,64,128]{3,2,1,0:T(8,128)(2,1)} %flow_hbm.1, bf16[1,64,64,128]{3,2,1,0:T(8,128)(2,1)} %wts_hbm.1), custom_call_target="tpu_custom_call" | custom-call | tf_op jit(solution)/shard_map/rotor/pallas_call | solution.py:518
  62.5 1.2 %copy.8 = f32[1,64]{1,0:T(1,128)} copy(f32[1,64]{1,0:T(1,128)} %rotor.1) | data formatting | bytes 512

commit v4 on v3

--- a/solution.py
+++ b/solution.py
@@ -49,7 +49,7 @@
 
 def main_kernel(
     dir_hbm, dest_hbm, bins_hbm, dens_hbm, flow_hbm, wts_hbm, out_ref,
-    dir_ref, dest_ref, bins_ref, dens, flow, list_vm, list_ref, lag_ref, C, S, R0, HC, LC, RA1, LA1, RA2, LA2, RA3, LA3, RA4, LA4,
+    dir_ref, dest_ref, bins_ref, dens_own, flow_own, dens_mate, flow_mate, list_vm, list_ref, lag_ref, C, S, R0, HC, LC, RA1, LA1, RA2, LA2, RA3, LA3, RA4, LA4,
     RB1, LB1, RB2, LB2, RB3, LB3, RB4, LB4, W, lag2, Z, G, M, HS, HR,
     ld_sem, s0, r0, sa1, ra1, sa2, ra2, sa3, ra3, sa4, ra4,
     sb1, rb1, sb2, rb2, sb3, rb3, sb4, rb4, sw, rw, sl, rl, sg, rg, sh, rh, met_y, met_mate,
@@ -86,14 +86,20 @@
         pltpu.make_async_copy(bins_hbm, bins_ref, ld_sem.at[5]),
         pltpu.make_async_copy(dir_hbm, dir_ref, ld_sem.at[6]),
     ]
-    loads = [
-        pltpu.make_async_copy(dens_hbm, dens.at[pl.ds(0, ROWS_DEV)], ld_sem.at[0]),
-        pltpu.make_async_copy(flow_hbm, flow.at[pl.ds(0, ROWS_DEV)], ld_sem.at[1]),
-        pltpu.make_async_copy(
-            wts_hbm.at[0, :, pl.ds(pl.multiple_of(c * 32, 32), 32), :], W.at[c], ld_sem.at[2]
-        ),
-    ]
-    for copy in small + loads:
+    def half(core):
+        return pl.ds(pl.multiple_of(core * 32, 32), 32)
+
+    def row_loads(core, dens, flow, at):
+        rows = pl.ds(0, ROWS_DEV)
+        return [
+            pltpu.make_async_copy(dens_hbm.at[:, half(core), :], dens.at[rows], ld_sem.at[at]),
+            pltpu.make_async_copy(flow_hbm.at[:, :, half(core), :], flow.at[rows], ld_sem.at[at + 1]),
+        ]
+
+    loads_mate = row_loads(1 - c, dens_mate, flow_mate, 0)
+    loads_own = row_loads(c, dens_own, flow_own, 7)
+    own_wts = pltpu.make_async_copy(wts_hbm.at[0, :, half(c), :], W.at[c], ld_sem.at[2])
+    for copy in small + loads_mate + loads_own + [own_wts]:
         copy.start()
     small[0].wait()
     small[1].wait()
@@ -131,8 +137,9 @@
         preferred_element_type=jnp.float32,
     ).astype(jnp.int32)
 
-    dens[ROWS_DEV] = jnp.zeros((64, 128), jnp.bfloat16)
-    flow[ROWS_DEV] = jnp.zeros((4, 64, 128), jnp.bfloat16)
+    for dens, flow in ((dens_own, flow_own), (dens_mate, flow_mate)):
+        dens[ROWS_DEV] = jnp.zeros((32, 128), jnp.bfloat16)
+        flow[ROWS_DEV] = jnp.zeros((4, 32, 128), jnp.bfloat16)
 
     pl.semaphore_wait(barrier, 7)
     for to in along_y:
@@ -144,36 +151,36 @@
     lag_copy = remote(lag_ref, lag2, sl, rl, mate)
 
     list_copy.wait()
-    loads[0].wait()
-    loads[1].wait()
+    for copy in loads_mate:
+        copy.wait()
 
     def core_copy(dx, dz):
         return remote(S.at[dx, dz], R0.at[dx, dz], s0.at[dx, dz], r0.at[dx, dz], mate)
 
-    def unit(dx, dz):
+    def unit(dx, dz, part):
         first = dev(dx, dz, 0)
+        target = C if part == 0 else S
+        dens, flow = (dens_own, flow_own) if part == 0 else (dens_mate, flow_mate)
         for j in range(2):
             rows = [list_ref[first + j, s] for s in range(SLOTS)]
-            for part in range(2):
-                target = C if part == 0 else S
-                for chunk in range(2):
-                    off = pl.multiple_of(((c + part) % 2) * 32 + chunk * 16, 16)
-                    span = pl.ds(off, 16)
-                    acc = None
-                    for r in rows:
-                        rho = dens[r, span, :].astype(jnp.float32)
-                        u = flow[r, 0, span, :].astype(jnp.float32)
-                        v = flow[r, 1, span, :].astype(jnp.float32)
-                        w = flow[r, 2, span, :].astype(jnp.float32)
-                        e = flow[r, 3, span, :].astype(jnp.float32)
-                        ru, rv, rw_ = rho * u, rho * v, rho * w
-                        terms = [ru * u, rv * v, rw_ * w, ru * v, ru * w, rv * w, e]
-                        acc = terms if acc is None else [p + q for p, q in zip(acc, terms)]
-                    sums = [acc[0] + acc[6], acc[1] + acc[6], acc[2] + acc[6], acc[3], acc[4], acc[5]]
-                    for tile, (ch, comp) in enumerate(TILES):
-                        if ch == chunk:
-                            target[dx, dz, place(j, tile)] = sums[comp]
-        core_copy(dx, dz).start()
+            for chunk in range(2):
+                span = pl.ds(chunk * 16, 16)
+                acc = None
+                for r in rows:
+                    rho = dens[r, span, :].astype(jnp.float32)
+                    u = flow[r, 0, span, :].astype(jnp.float32)
+                    v = flow[r, 1, span, :].astype(jnp.float32)
+                    w = flow[r, 2, span, :].astype(jnp.float32)
+                    e = flow[r, 3, span, :].astype(jnp.float32)
+                    ru, rv, rw_ = rho * u, rho * v, rho * w
+                    terms = [ru * u, rv * v, rw_ * w, ru * v, ru * w, rv * w, e]
+                    acc = terms if acc is None else [p + q for p, q in zip(acc, terms)]
+                sums = [acc[0] + acc[6], acc[1] + acc[6], acc[2] + acc[6], acc[3], acc[4], acc[5]]
+                for tile, (ch, comp) in enumerate(TILES):
+                    if ch == chunk:
+                        target[dx, dz, place(j, tile)] = sums[comp]
+        if part == 1:
+            core_copy(dx, dz).start()
 
     def combine(dx, dz, spans, send):
         for lo, hi, came in spans:
@@ -332,27 +339,45 @@
     def group(g, carry):
         dz = far_first(g, NZ)
 
-        def step(k, inner):
-            unit(far_first(k, NX), dz)
+        def across(k, inner):
+            unit(far_first(k, NX), dz, 1)
             return inner
 
-        lax.fori_loop(0, NX, step, 0)
-
-        @pl.when(g >= 1)
+        def ahead(k, inner):
+            unit(far_first(k, NX), far_first(g + 1, NZ), 1)
+            return inner
+
+        def own(k, inner):
+            unit(far_first(k, NX), dz, 0)
+            return inner
+
+        @pl.when(g == 0)
         def _():
-            finish(g - 1)
-
-        @pl.when(g == 3)
+            lax.fori_loop(0, NX, across, 0)
+            for copy in loads_own:
+                copy.wait()
+
+        @pl.when(g < NZ - 1)
         def _():
-            def send(k, inner):
-                ev_b2(0, far_first(k, NX))
-                return inner
-
-            lax.fori_loop(0, NX, send, 0)
-
-        @pl.when(g >= 4)
+            lax.fori_loop(0, NX, ahead, 0)
+
+        lax.fori_loop(0, NX, own, 0)
+
+        finish(g)
+
+        for step in range(2):
+
+            @pl.when(g == 2 + 3 * step)
+            def _(step=step):
+                def send(k, inner):
+                    ev_b2(step, far_first(k, NX))
+                    return inner
+
+                lax.fori_loop(0, NX, send, 0)
+
+        @pl.when(g >= 3)
         def _():
-            ev_a2(far_first(g - 4, NZ))
+            ev_a2(far_first(g - 3, NZ))
 
         return carry
 
@@ -361,33 +386,27 @@
     lag_copy.start()
     pl.semaphore_wait(met_y, 2)
     pl.semaphore_signal(met_mate, inc=1, device_id=(mate, yy), device_id_type=MESH)
-    finish(NZ - 1)
-    ev_b2(1, 2)
-    ev_b2(1, 1)
-    ev_b2(1, 3)
-    ev_a2(6)
-    ev_b2(1, 0)
-    ev_a2(1)
     ev_b2(2, 2)
     ev_ra2(4)
     ev_b2(2, 1)
+    ev_a2(1)
     ev_ra2(3)
     ev_b2(2, 3)
+    ev_ra2(5)
     ev_b2(2, 0)
-    ev_ra2(5)
     ev_rb2(2)
     ev_a2(7)
     ev_a2(0)
     ev_ra2(2)
     ev_ra2(6)
-    ev_ra2(1)
     ev_rb2(1)
     ev_rb2(3)
+    ev_ra2(1)
     ev_ra2(7)
+    ev_rb2(0)
     ev_ra2(0)
-    ev_rb2(0)
-
-    loads[2].wait()
+
+    own_wts.wait()
     small[2].wait()
     wts_copy.wait()
     lag_copy.wait()
@@ -419,8 +438,8 @@
     Z[1] = jnp.where(low, pltpu.roll(cols[0], 64, 1), cols[1])
     pl.semaphore_wait(met_mate, 1)
     mine = yy * 2 + c
-    for dc in range(2):
-        for dy in range(NY):
+    for dy in (2, 1, 3, 0):
+        for dc in range(2):
             core = (c + dc) % 2
             if dy or dc:
                 remote(Z.at[core], G.at[mine], sg, rg, chip * 2 + core, (yy + dy) % NY).start()
@@ -446,15 +465,13 @@
     for i in range(32):
         HS[i] = M[pl.ds(i, 1), :]
 
-    def m_h(r):
-        to = dev(r // NZ, r % NZ, c)
-        return remote(HS.at[to // 2], HR.at[r - 1], sh, rh, to)
-
-    def send(r, carry):
-        m_h(r).start()
+    def send(i, carry):
+        dx, dz = far_first(i // NZ, NX), far_first(i % NZ, NZ)
+        to = dev(dx, dz, c)
+        remote(HS.at[to // 2], HR.at[dx * NZ + dz - 1], sh, rh, to).start()
         return carry
 
-    lax.fori_loop(1, 32, send, 0)
+    lax.fori_loop(0, NX * NZ - 1, send, 0)
 
     wait_all = [core_copy(i, j) for i in range(NX) for j in range(NZ)]
     wait_all += [m_a1(d, j) for d in range(2) for j in range(NZ)]
@@ -485,8 +502,10 @@
         pltpu.SMEM((3, 64), f32),
         vm((1, ROWS_DEV), jnp.int32),
         vm((1, 64), jnp.int32),
-        vm((ROWS_DEV + 1, 64, 128), bf16),
-        vm((ROWS_DEV + 1, 4, 64, 128), bf16),
+        vm((ROWS_DEV + 1, 32, 128), bf16),
+        vm((ROWS_DEV + 1, 4, 32, 128), bf16),
+        vm((ROWS_DEV + 1, 32, 128), bf16),
+        vm((ROWS_DEV + 1, 4, 32, 128), bf16),
         vm((64, 128), jnp.int32),
         pltpu.SMEM((64, 128), jnp.int32),
         vm((8, 128), jnp.int32),
@@ -509,7 +528,7 @@
         vm((128, 128), f32),
         vm((32, 1, 128), f32),
         vm((31, 1, 128), f32),
-        dma((7,)),
+        dma((9,)),
     ]
     scratch += [dma((NX, NZ))] * 2
     for shape in ((2, NZ), (2, NZ), (2,), (2, 3), (2, NX), (2, 3, NX), (2,), (2,)):

time: 63.7 us -> 60.9 us (0.956)
  Pallas kernels: 62.5 us -> 59.6 us
    pallas_call x1, Pallas kernels: 62.5 us -> 59.6 us  [body(): pl.pallas_call(main_kernel, out_shape=jax.ShapeDtypeStruct((1, 64), f32),...]
where the time goes in v4:
time: 60.9 us; the launch traced here: 60.8 us
  Pallas kernels  59.6 us (98%)
  local copies, waits for them, and re-layouts  1.19 us (2%)
    pallas_call x1, Pallas kernels, body(): pl.pallas_call(main_kernel, out_shape=jax.ShapeDtypeStruct((1, 64), f32),...  59.6 us

profile of v4, /device:TPU:1, one launch (start us, length us, event | category | flops | bytes accessed | tf_op | source)
XLA Modules:
  0.0 60.8 jit_solution(5233272781404874852)
XLA Ops:
  0.0 59.6 %rotor.1 = f32[1,64]{1,0:T(1,128)} custom-call(f32[3,64]{1,0:T(4,128)} %bitcast.3, s32[1,96]{1,0:T(1,128)} %bitcast.4, s32[1,64]{1,0:T(1,128)} %bitcast.5, bf16[96,64,128]{2,1,0:T(8,128)(2,1)} %dens_hbm.1, bf16[96,4,64,128]{3,2,1,0:T(8,128)(2,1)} %flow_hbm.1, bf16[1,64,64,128]{3,2,1,0:T(8,128)(2,1)} %wts_hbm.1), custom_call_target="tpu_custom_call" | custom-call | tf_op jit(solution)/shard_map/rotor/pallas_call | solution.py:537
  59.6 1.2 %copy.8 = f32[1,64]{1,0:T(1,128)} copy(f32[1,64]{1,0:T(1,128)} %rotor.1) | data formatting | bytes 512

commit v5 on v4

--- a/solution.py
+++ b/solution.py
@@ -387,18 +387,18 @@
     pl.semaphore_wait(met_y, 2)
     pl.semaphore_signal(met_mate, inc=1, device_id=(mate, yy), device_id_type=MESH)
     ev_b2(2, 2)
+    ev_b2(2, 1)
     ev_ra2(4)
-    ev_b2(2, 1)
     ev_a2(1)
+    ev_b2(2, 3)
     ev_ra2(3)
-    ev_b2(2, 3)
+    ev_b2(2, 0)
     ev_ra2(5)
-    ev_b2(2, 0)
     ev_rb2(2)
     ev_a2(7)
-    ev_a2(0)
     ev_ra2(2)
     ev_ra2(6)
+    ev_a2(0)
     ev_rb2(1)
     ev_rb2(3)
     ev_ra2(1)
@@ -431,7 +431,7 @@
         return tuple(new)
 
     zero = jnp.zeros((16, 128), jnp.float32)
-    cols = lax.fori_loop(0, 64, project, (zero, zero), unroll=8)
+    cols = lax.fori_loop(0, 64, project, (zero, zero), unroll=16)
 
     low = lane16 < 64
     Z[0] = jnp.where(low, cols[0], pltpu.roll(cols[1], 64, 1))

time: 60.9 us -> 60.6 us (level)
  no operation moved by 1% of the time
where the time goes in v5:
time: 60.6 us; the launch traced here: 60.5 us
  Pallas kernels  59.3 us (98%)
  local copies, waits for them, and re-layouts  1.19 us (2%)
    pallas_call x1, Pallas kernels, body(): pl.pallas_call(main_kernel, out_shape=jax.ShapeDtypeStruct((1, 64), f32),...  59.3 us

profile of v5, /device:TPU:1, one launch (start us, length us, event | category | flops | bytes accessed | tf_op | source)
XLA Modules:
  0.0 60.5 jit_solution(18034217876002706323)
XLA Ops:
  0.0 59.3 %rotor.1 = f32[1,64]{1,0:T(1,128)} custom-call(f32[3,64]{1,0:T(4,128)} %bitcast.3, s32[1,96]{1,0:T(1,128)} %bitcast.4, s32[1,64]{1,0:T(1,128)} %bitcast.5, bf16[96,64,128]{2,1,0:T(8,128)(2,1)} %dens_hbm.1, bf16[96,4,64,128]{3,2,1,0:T(8,128)(2,1)} %flow_hbm.1, bf16[1,64,64,128]{3,2,1,0:T(8,128)(2,1)} %wts_hbm.1), custom_call_target="tpu_custom_call" | custom-call | tf_op jit(solution)/shard_map/rotor/pallas_call | solution.py:537
  59.3 1.2 %copy.8 = f32[1,64]{1,0:T(1,128)} copy(f32[1,64]{1,0:T(1,128)} %rotor.1) | data formatting | bytes 512
